TPU v7x, 512 devices: a whole 4x8x8 slice. The times are simulated.
512 devices in a mesh: grp: 8 (over z_lo, x), tile: 64 (over y, z_hi, core).
Axes of the slice: x: 4, y: 8, z: 8 (z_hi: 4, z_lo: 2; z = z_hi * 2 + z_lo), core: 2. Of those that a mesh axis runs over, the one named last changes fastest.
Arguments:
- pixels: bfloat16 [512, 128, 3, 256], P(('grp', 'tile')), parts along dimension 0, may hold values from -6 to 6
- patch_weight: bfloat16 [768, 1024], P('tile'), may hold values from -0.21875 to 0.21875
- qkv_weight: bfloat16 [1024, 1536], P('tile'), may hold values from -2.0625 to 2.0625
- out_weight: bfloat16 [512, 1024], P('tile'), may hold values from -0.25 to 0.25
- reward_head: float32 [1024], replicated, may hold values from -4 to 4
- conv_weight: bfloat16 [3, 3, 48, 3], replicated, may hold values from -1.25 to 1.25
Outputs:
- rewards: float32 [512], P(('grp', 'tile')), parts along dimension 0
- act_grad: bfloat16 [512, 128, 48, 256], P('grp', 'tile'), parts along dimension 0
There are 8 independent parts, one for each index of `grp`. A program takes and returns all parts, laid end to end along the dimension named above; an argument that names none is the same for every part. Nothing has to cross between parts.
All inputs are finite; a program needn't handle non-finite values.
Results may differ from a plain program's by a relative error of at most 0.02.
Values may be sent and summed in bfloat16 or wider, within the bound.
No kernel may reach another device: no remote copies, remote signals or barrier semaphores. Data moves between devices by JAX's collectives and lax.ppermute only.
A program may use at most 64 MiB of HBM per device.

v0:
```python
import jax
import jax.numpy as jnp
from jax import lax
from jax.sharding import PartitionSpec as P

D = 1024
HEADS = 8
HEAD_DIM = 64
PATCH = 16
PDIM = 768
LOSS_SCALE = 1024.0
NORM_EPSILON = 1e-05


def extended(value, sides, width):
    for axis, dim in sides:
        devices, length = (lax.axis_size(axis), value.shape[dim])
        up = [(i, (i + 1) % devices) for i in range(devices - 1)]
        down = [(j, i) for i, j in up]
        last = lax.slice_in_dim(value, length - width, length, axis=dim)
        first = lax.slice_in_dim(value, 0, width, axis=dim)
        before = lax.ppermute(last, axis, up)
        after = lax.ppermute(first, axis, down)
        value = jnp.concatenate([before, value, after], axis=dim)
    return value


def normalize(values_in):
    average = jnp.mean(values_in, -1, keepdims=True)
    centred = values_in - average
    inverse_scale = lax.rsqrt(jnp.mean(centred * centred, -1, keepdims=True) + NORM_EPSILON)
    return (centred * inverse_scale, inverse_scale)


def norm_back(grad_in, normed, inverse_scale):
    return inverse_scale * (
        grad_in
        - jnp.mean(grad_in, -1, keepdims=True)
        - normed * jnp.mean(grad_in * normed, -1, keepdims=True)
    )


def to_patch_rows(pixels):
    frame_count, row_count, _, col_count = pixels.shape
    blocks = pixels.reshape(frame_count, row_count // PATCH, PATCH, 3, col_count // PATCH, PATCH)
    blocks = blocks.transpose(0, 1, 4, 3, 2, 5)
    return blocks.reshape(frame_count, row_count // PATCH * (col_count // PATCH), 3 * PATCH * PATCH)


def from_patch_rows(patches, row_count, col_count):
    frame_count = patches.shape[0]
    blocks = patches.reshape(frame_count, row_count // PATCH, col_count // PATCH, 3, PATCH, PATCH)
    blocks = blocks.transpose(0, 1, 4, 3, 2, 5)
    return blocks.reshape(frame_count, row_count, 3, col_count)


def attend_forward(spread, full_qkv):
    frame_count, local_count, model_width = spread.shape
    score_scale = HEAD_DIM ** (-0.5)
    first_normed, first_scale = normalize(spread.astype(jnp.float32))
    projected = jnp.dot(
        first_normed.astype(jnp.bfloat16).reshape(-1, model_width),
        full_qkv,
        preferred_element_type=jnp.float32,
    )
    projected = projected.astype(jnp.bfloat16).reshape(frame_count, local_count, 3, HEADS, HEAD_DIM)
    query_rows = projected[:, :, 0]
    key_rows = projected[:, :, 1]
    value_rows = projected[:, :, 2]
    scores = (
        jnp.einsum("iphd,jphd->phij", query_rows, key_rows, preferred_element_type=jnp.float32)
        * score_scale
    )
    attn_probs = jax.nn.softmax(scores, axis=-1)
    probs_rounded = attn_probs.astype(jnp.bfloat16)
    attended = jnp.einsum(
        "phij,jphd->iphd", probs_rounded, value_rows, preferred_element_type=jnp.float32
    )
    attended = attended.astype(jnp.bfloat16).reshape(frame_count, local_count, HEADS * HEAD_DIM)
    return (
        first_normed,
        first_scale,
        query_rows,
        key_rows,
        value_rows,
        attn_probs,
        probs_rounded,
        attended,
    )


def attend_backward(grad_spread, saved, back_qkv):
    first_normed, first_scale, query_rows, key_rows, value_rows, attn_probs, probs_rounded, _ = (
        saved
    )
    frame_count, local_count = (first_normed.shape[0], first_normed.shape[1])
    score_scale = HEAD_DIM ** (-0.5)
    grad_heads = grad_spread.reshape(frame_count, local_count, HEADS, HEAD_DIM)
    grad_probs = jnp.einsum(
        "iphd,jphd->phij", grad_heads, value_rows, preferred_element_type=jnp.float32
    )
    grad_value = jnp.einsum(
        "phij,iphd->jphd", probs_rounded, grad_heads, preferred_element_type=jnp.float32
    ).astype(jnp.bfloat16)
    row_delta = jnp.sum(attn_probs * grad_probs, -1, keepdims=True)
    grad_scores = (attn_probs * (grad_probs - row_delta) * score_scale).astype(jnp.bfloat16)
    grad_query = jnp.einsum(
        "phij,jphd->iphd", grad_scores, key_rows, preferred_element_type=jnp.float32
    ).astype(jnp.bfloat16)
    grad_key = jnp.einsum(
        "phij,iphd->jphd", grad_scores, query_rows, preferred_element_type=jnp.float32
    ).astype(jnp.bfloat16)
    grad_proj = jnp.stack([grad_query, grad_key, grad_value], 2).reshape(-1, 3 * HEADS * HEAD_DIM)
    grad_first = jnp.dot(grad_proj, back_qkv.T, preferred_element_type=jnp.float32)
    grad_first = grad_first.reshape(first_normed.shape)
    return norm_back(grad_first, first_normed, first_scale).astype(jnp.bfloat16)


def on_device(pixels, patch_weight, qkv_weight, out_weight, reward_head, conv_weight):
    local_frames, row_count, _, col_count = pixels.shape
    model_width = D
    inner_width = HEADS * HEAD_DIM
    full_patch, full_qkv, full_out = (
        lax.all_gather(patch_weight, "tile", axis=0, tiled=True),
        lax.all_gather(qkv_weight, "tile", axis=0, tiled=True),
        lax.all_gather(out_weight, "tile", axis=0, tiled=True),
    )
    patches = to_patch_rows(pixels)
    patch_count = patches.shape[1]
    spread_patches = lax.all_to_all(patches, "tile", split_axis=1, concat_axis=0, tiled=True)
    frame_count, local_count = (spread_patches.shape[0], spread_patches.shape[1])
    embedded = jnp.dot(
        spread_patches.reshape(-1, PDIM), full_patch, preferred_element_type=jnp.float32
    )
    embedded = embedded.astype(jnp.bfloat16).reshape(frame_count, local_count, model_width)
    saved = attend_forward(embedded, full_qkv)
    hidden = embedded.astype(jnp.float32) + jnp.dot(
        saved[7].reshape(-1, inner_width), full_out, preferred_element_type=jnp.float32
    ).reshape(embedded.shape)
    second_normed, second_scale = normalize(hidden)
    partial_sums = jnp.sum(jnp.sum(second_normed * reward_head, -1), -1)
    all_rewards = lax.psum(partial_sums, "tile") / patch_count
    rewards = lax.dynamic_slice_in_dim(
        all_rewards, lax.axis_index("tile") * local_frames, local_frames
    )
    frame_coeff = -LOSS_SCALE * jax.nn.sigmoid(-all_rewards)
    grad_second = frame_coeff[:, None, None] * reward_head / patch_count
    grad_hidden = norm_back(grad_second, second_normed, second_scale)
    hidden_rounded = grad_hidden.astype(jnp.bfloat16)
    back_patch, back_qkv, back_out = (
        lax.all_gather(patch_weight, "tile", axis=0, tiled=True),
        lax.all_gather(qkv_weight, "tile", axis=0, tiled=True),
        lax.all_gather(out_weight, "tile", axis=0, tiled=True),
    )
    grad_attended = jnp.dot(
        hidden_rounded.reshape(-1, model_width), back_out.T, preferred_element_type=jnp.float32
    )
    grad_attended = grad_attended.astype(jnp.bfloat16).reshape(
        hidden.shape[0], hidden.shape[1], inner_width
    )
    grad_embed = attend_backward(grad_attended, saved, back_qkv)
    grad_total = (grad_hidden + grad_embed.astype(jnp.float32)).astype(jnp.bfloat16)
    grad_patches = jnp.dot(
        grad_total.reshape(-1, model_width), back_patch.T, preferred_element_type=jnp.float32
    )
    grad_patches = grad_patches.astype(jnp.bfloat16).reshape(hidden.shape[0], hidden.shape[1], PDIM)
    home_patches = lax.all_to_all(grad_patches, "tile", split_axis=0, concat_axis=1, tiled=True)
    grad_pixels = from_patch_rows(home_patches, row_count, col_count)
    row_grad = lax.all_to_all(grad_pixels, "tile", split_axis=1, concat_axis=0, tiled=True)
    tile_rows = row_grad.shape[1]
    padded = extended(row_grad, (("tile", 1),), 1)
    padded = jnp.pad(padded, ((0, 0), (0, 0), (0, 0), (1, 1)))
    pieces = [
        padded[:, 2 - row_off : 2 - row_off + tile_rows, :, 2 - col_off : 2 - col_off + col_count]
        for row_off in range(3)
        for col_off in range(3)
    ]
    stacked = jnp.stack(pieces, 2).reshape(row_grad.shape[0], tile_rows, 27, col_count)
    kernel = conv_weight.transpose(0, 1, 3, 2).reshape(27, -1)
    act_grad = jnp.einsum(
        "fykx,kc->fycx", stacked, kernel, preferred_element_type=jnp.float32
    ).astype(jnp.bfloat16)
    return (rewards, act_grad)


def solution(mesh):
    in_specs = (
        P(("grp", "tile"), None, None, None),
        P("tile", None),
        P("tile", None),
        P("tile", None),
        P(),
        P(),
    )
    out_specs = (P(("grp", "tile")), P("grp", "tile", None, None))
    return jax.shard_map(
        on_device, mesh=mesh, in_specs=in_specs, out_specs=out_specs, check_vma=False
    )
```

profile of v0, /device:TPU:1, one launch (start us, length us, event | category | flops | bytes accessed | tf_op | source)
XLA Modules:
  0.0 508.4 jit_solution(12765785373744496446)
XLA Ops:
  8.6 2.1 reshape.213
  12.8 1.8 reduce.4
  15.3 17.6 %all-to-all-start = ((bf16[64,2,768]{2,1,0:T(2,128)(2,1)}), bf16[64,2,768]{2,1,0:T(2,128)(2,1)S(1)}, u32[]{:S(2)}, u32[]{:S(2)}) async-start(bf16[64,2,768]{2,1,0:T(2,128)(2,1)} %reshape.233), calls=%async_computation | async-start | bytes 393216 | tf_op jit(solution)/shard_map/all_to_all | solution.py:130
  33.7 14.1 %all-to-all-done = bf16[64,2,768]{2,1,0:T(2,128)(2,1)S(1)} async-done(((bf16[64,2,768]{2,1,0:T(2,128)(2,1)}), bf16[64,2,768]{2,1,0:T(2,128)(2,1)S(1)}, u32[]{:S(2)}, u32[]{:S(2)}) %all-to-all-start) | async-done | bytes 196640 | tf_op jit(solution)/shard_map/all_to_all | solution.py:130
  47.9 55.3 %all-gather.9.cloned.1.call-done = bf16[64,12,1024]{2,1,0:T(8,128)(2,1)} async-done(((bf16[1,12,1024]{2,1,0:T(8,128)(2,1)}), bf16[64,12,1024]{2,1,0:T(8,128)(2,1)}) %all-gather.9.cloned.1.call-update) | async-done | bytes 1572880 | tf_op jit(solution)/shard_map/all_gather | solution.py:124
  103.2 2.5 reshape.226
  107.7 81.3 %all-gather.5.cloned.1.call-done = bf16[1024,1536]{1,0:T(8,128)(2,1)} async-done(((bf16[16,1536]{1,0:T(8,128)(2,1)}), bf16[1024,1536]{1,0:T(8,128)(2,1)}) %all-gather.5.cloned.1.call-update) | async-done | bytes 3145744 | tf_op jit(solution)/shard_map/all_gather | solution.py:125
  189.0 2.5 convolution_convert_fusion
  195.4 76.6 %all-gather.7.cloned.1.call-done = bf16[512,1024]{1,0:T(8,128)(2,1)} async-done(((bf16[8,1024]{1,0:T(8,128)(2,1)}), bf16[512,1024]{1,0:T(8,128)(2,1)}) %all-gather.7.cloned.1.call-update) | async-done | bytes 1048592 | tf_op jit(solution)/shard_map/all_gather | solution.py:126
  272.0 1.7 fusion.55
  274.2 138.3 %psum.7 = f32[64]{0:T(128)S(1)} all-reduce(f32[64]{0:T(128)S(1)} %multiply_reduce_fusion.3), channel_id=1, replica_groups=mesh['grp'=8,'tile'=64] {'tile'}, use_global_device_ids=true, to_apply=%region_7.0 | all-reduce | flops 64 | bytes 512 | tf_op jit(solution)/shard_map/psum | solution.py:142
  414.6 1.7 convolution_convert_fusion.7
  417.9 2.7 fusion.13
  420.6 2.6 fusion.14
  426.0 1.8 dot_general.54
  427.8 3.2 fusion.50
  432.6 23.5 %all_to_all.30 = bf16[64,2,768]{2,1,0:T(2,128)(2,1)S(1)} all-to-all(bf16[64,2,768]{2,1,0:T(2,128)(2,1)S(1)} %reshape.219), channel_id=1, replica_groups=mesh['grp'=8,'tile'=64] {'tile'}, dimensions={0} | all-to-all | bytes 393216 | tf_op jit(solution)/shard_map/all_to_all | solution.py:167
  457.6 1.8 reshape.231
  459.4 19.2 %all_to_all.31 = bf16[1,128,3,256]{3,2,0,1:T(4,128)(2,1)S(1)} all-to-all(bf16[1,128,3,256]{3,2,0,1:T(4,128)(2,1)S(1)} %reshape.231), channel_id=1, replica_groups=mesh['grp'=8,'tile'=64] {'tile'}, dimensions={1} | all-to-all | bytes 393216 | tf_op jit(solution)/shard_map/all_to_all | solution.py:169
  479.1 3.3 collective-permute-start
  482.4 2.1 collective-permute-start.1
  485.2 8.7 %collective-permute-done.1 = bf16[64,1,3,256]{3,1,0,2:T(2,128)(2,1)S(1)} collective-permute-done((bf16[64,1,3,256]{3,1,0,2:T(2,128)(2,1)S(1)}, bf16[64,1,3,256]{3,1,0,2:T(2,128)(2,1)S(1)}, u32[]{:S(2)}, u32[]{:S(2)}) %collective-permute-start.1) | collective-permute-done | bytes 98336 | tf_op jit(solution)/shard_map/ppermute | solution.py:23
  493.8 1.8 select_maximum_fusion
  498.8 3.1 convert_bitcast_fusion
  (90 shorter events, 25.1 us)
Async XLA Ops:
  7.2 96.0 %all-gather.9.cloned.1.call-start = ((), (), s32[]{:S(2)}) async-start(), calls=%async_computation.5 | async-start | bytes 2129920 | tf_op jit(solution)/shard_map/all_gather | solution.py:124
  7.9 181.1 %all-gather.5.cloned.1.call-start = ((), (), s32[]{:S(2)}) async-start(), calls=%async_computation.3 | async-start | bytes 3194880 | tf_op jit(solution)/shard_map/all_gather | solution.py:125
  15.3 32.4 %all-to-all-start = ((bf16[64,2,768]{2,1,0:T(2,128)(2,1)}), bf16[64,2,768]{2,1,0:T(2,128)(2,1)S(1)}, u32[]{:S(2)}, u32[]{:S(2)}) async-start(bf16[64,2,768]{2,1,0:T(2,128)(2,1)} %reshape.233), calls=%async_computation | async-start | bytes 393216 | tf_op jit(solution)/shard_map/all_to_all | solution.py:130
  32.9 239.1 %all-gather.7.cloned.1.call-start = ((), (), s32[]{:S(2)}) async-start(), calls=%async_computation.4 | async-start | bytes 1064960 | tf_op jit(solution)/shard_map/all_gather | solution.py:126
  194.6 0.6 copy-start.10
  194.6 77.4 %copy-start.9 = (f32[2,8,64,64]{2,3,1,0:T(8,128)}, f32[2,8,64,64]{2,3,1,0:T(8,128)S(1)}, u32[]{:S(2)}) copy-start(f32[2,8,64,64]{2,3,1,0:T(8,128)S(1)} %get-tuple-element.16) | copy-start | bytes 786436
  195.4 78.5 %copy-start.5 = (f32[1024]{0:T(1024)S(1)}, f32[1024]{0:T(1024)}, u32[]{:S(2)}) copy-start(f32[1024]{0:T(1024)} %param.10) | copy-start | bytes 12292
  413.3 0.7 copy-start
  416.8 3.7 copy-start.2
  416.8 3.7 copy-start.11
  423.1 1.4 copy-start.3
  423.1 1.4 copy-start.4
  424.7 3.0 copy-start.7
  427.8 3.2 copy-start.1
  457.6 26.9 %copy-start.6 = (bf16[3,3,48,3]{2,3,1,0:T(4,128)(2,1)S(1)}, bf16[3,3,48,3]{2,3,1,0:T(4,128)(2,1)}, u32[]{:S(2)}) copy-start(bf16[3,3,48,3]{2,3,1,0:T(4,128)(2,1)} %param.11) | copy-start | bytes 7780
  457.6 26.9 %copy-start.8 = (f32[64]{0:T(128)S(1)}, f32[64]{0:T(128)}, u32[]{:S(2)}) copy-start(f32[64]{0:T(128)} %get-tuple-element.12) | copy-start | bytes 772
  479.1 6.1 %collective-permute-start = (bf16[64,1,3,256]{3,1,0,2:T(2,128)(2,1)S(1)}, bf16[64,1,3,256]{3,1,0,2:T(2,128)(2,1)S(1)}, u32[]{:S(2)}, u32[]{:S(2)}) collective-permute-start(bf16[64,1,3,256]{3,1,0,2:T(2,128)(2,1)S(1)} %get-tuple-element.7), channel_id=1, source_target_pairs={{0,1},{1,2},{2,3},{3,4},{4,5},{5,6},{6,7},{7,8},{8,9},{9,10},{10,1... | collective-permute-start | bytes 294920 | tf_op jit(solution)/shard_map/ppermute | solution.py:22
  482.4 11.5 %collective-permute-start.1 = (bf16[64,1,3,256]{3,1,0,2:T(2,128)(2,1)S(1)}, bf16[64,1,3,256]{3,1,0,2:T(2,128)(2,1)S(1)}, u32[]{:S(2)}, u32[]{:S(2)}) collective-permute-start(bf16[64,1,3,256]{3,1,0,2:T(2,128)(2,1)S(1)} %get-tuple-element.8), channel_id=1, source_target_pairs={{1,0},{2,1},{3,2},{4,3},{5,4},{6,5},{7,6},{8,7},{9,8},{10,9},{11,1... | collective-permute-start | bytes 294920 | tf_op jit(solution)/shard_map/ppermute | solution.py:23
Sparse Core Ops, SparseCore 0:
  11.3 91.8 all-gather.8
  106.5 82.4 all-gather.4
  192.3 79.6 all-gather.6
where the time goes:
time: 509 us; the launch traced here: 508 us
  waiting for transfers between devices  238 us (47%)
  blocking collectives  181 us (36%)
  starting transfers between devices  23.1 us (5%)
  matrix products  22.6 us (4%)
  local copies, waits for them, and re-layouts  22.4 us (4%)
  between operations  14.2 us (3%)
  other arithmetic  7.14 us (1%)
    psum x1, blocking collectives, on_device(): all_rewards = lax.psum(partial_sums, 'tile') / patch_count  138 us
    all_gather x1, waiting for transfers between devices, on_device(): lax.all_gather(qkv_weight, 'tile', axis=0, tiled=True)  81.3 us
    all_gather x1, waiting for transfers between devices, on_device(): lax.all_gather(out_weight, 'tile', axis=0, tiled=True)  76.6 us
    all_gather x1, waiting for transfers between devices, on_device(): lax.all_gather(patch_weight, 'tile', axis=0, tiled=True)  55.3 us
    all_to_all x1, blocking collectives, on_device(): lax.all_to_all(grad_patches, 'tile', split_axis=0, concat_axis=1, tiled=T...  23.5 us
    all_to_all x1, blocking collectives, on_device(): lax.all_to_all(grad_pixels, 'tile', split_axis=1, concat_axis=0, tiled=True)  19.2 us
    all_to_all x1, starting transfers between devices, on_device(): lax.all_to_all(patches, 'tile', split_axis=1, concat_axis=0, tiled=True)  17.6 us
    all_to_all x1, waiting for transfers between devices, on_device(): lax.all_to_all(patches, 'tile', split_axis=1, concat_axis=0, tiled=True)  14.1 us
  transfers between devices with their start and end apart: 6, of which 5 were waited for; matrix products, arithmetic and copies ran while one was open for 3% of the time, Pallas kernels for 0%

commit v1 on v0

--- a/solution.py
+++ b/solution.py
@@ -121,7 +121,9 @@
     model_width = D
     inner_width = HEADS * HEAD_DIM
     full_patch, full_qkv, full_out = (
-        lax.all_gather(patch_weight, "tile", axis=0, tiled=True),
+        jnp.concatenate(
+            lax.all_to_all(jnp.stack([patch_weight] * lax.axis_size("tile")), "tile", 0, 0), axis=0
+        ),
         lax.all_gather(qkv_weight, "tile", axis=0, tiled=True),
         lax.all_gather(out_weight, "tile", axis=0, tiled=True),
     )

time: 509 us -> 540 us (1.061)
  blocking collectives: 181 us -> 213 us
  starting transfers between devices: 23.1 us -> 10 us
  waiting for transfers between devices: 238 us -> 246 us
    all_to_all x1, waiting for transfers between devices: 14.1 us -> 51 us  [on_device(): lax.all_to_all(jnp.stack([patch_weight] * lax.axis_size('tile')), 'tile',...]
    all_gather x1, waiting for transfers between devices: 55.3 us -> 21.2 us  [on_device(): lax.all_gather(patch_weight, 'tile', axis=0, tiled=True)]
    all_to_all x0 -> x1, blocking collectives: none -> 32 us  [on_device(): lax.all_to_all(patches, 'tile', split_axis=1, concat_axis=0, tiled=True)]
    all_to_all x1, starting transfers between devices: 17.6 us -> 4.48 us  [on_device(): lax.all_to_all(jnp.stack([patch_weight] * lax.axis_size('tile')), 'tile',...]
  transfers between devices with their start and end apart: 6 -> 6, of which waited for: 5 -> 5; matrix products, arithmetic and copies ran while one was open for 3% -> 4% of each run, Pallas kernels for 0% -> 0%
where the time goes in v1:
time: 540 us; the launch traced here: 539 us
  waiting for transfers between devices  246 us (46%)
  blocking collectives  213 us (39%)
  local copies, waits for them, and re-layouts  24.5 us (5%)
  matrix products  24 us (4%)
  between operations  14.2 us (3%)
  starting transfers between devices  10 us (2%)
  other arithmetic  7.14 us (1%)
    psum x1, blocking collectives, on_device(): all_rewards = lax.psum(partial_sums, 'tile') / patch_count  138 us
    all_gather x1, waiting for transfers between devices, on_device(): lax.all_gather(qkv_weight, 'tile', axis=0, tiled=True)  86.5 us
    all_gather x1, waiting for transfers between devices, on_device(): lax.all_gather(out_weight, 'tile', axis=0, tiled=True)  76.6 us
    all_to_all x1, waiting for transfers between devices, on_device(): lax.all_to_all(jnp.stack([patch_weight] * lax.axis_size('tile')), 'tile',...  51 us
    all_to_all x1, blocking collectives, on_device(): lax.all_to_all(patches, 'tile', split_axis=1, concat_axis=0, tiled=True)  32 us
    all_to_all x1, blocking collectives, on_device(): lax.all_to_all(grad_patches, 'tile', split_axis=0, concat_axis=1, tiled=T...  23.5 us
    all_gather x1, waiting for transfers between devices, on_device(): lax.all_gather(patch_weight, 'tile', axis=0, tiled=True)  21.2 us
    all_to_all x1, blocking collectives, on_device(): lax.all_to_all(grad_pixels, 'tile', split_axis=1, concat_axis=0, tiled=True)  19.2 us
  transfers between devices with their start and end apart: 6, of which 5 were waited for; matrix products, arithmetic and copies ran while one was open for 4% of the time, Pallas kernels for 0%

profile of v1, /device:TPU:1, one launch (start us, length us, event | category | flops | bytes accessed | tf_op | source)
XLA Modules:
  0.0 538.9 jit_solution(13860853776164044633)
XLA Ops:
  8.6 2.1 reshape.218
  12.8 1.8 reduce.4
  14.7 32.0 %all_to_all.35 = bf16[64,2,768]{2,1,0:T(2,128)(2,1)S(1)} all-to-all(bf16[64,2,768]{2,1,0:T(2,128)(2,1)S(1)} %reshape.239), channel_id=1, replica_groups=mesh['grp'=8,'tile'=64] {'tile'}, dimensions={0} | all-to-all | bytes 393216 | tf_op jit(solution)/shard_map/all_to_all | solution.py:132
  48.3 4.5 all-to-all-start.1
  53.7 51.0 %all-to-all-done.1 = bf16[64,12,1024]{2,1,0:T(8,128)(2,1)S(1)} async-done(((bf16[64,12,1024]{2,1,0:T(8,128)(2,1)}), bf16[64,12,1024]{2,1,0:T(8,128)(2,1)S(1)}, u32[]{:S(2)}, u32[]{:S(2)}) %all-to-all-start.1) | async-done | bytes 1572896 | tf_op jit(solution)/shard_map/all_to_all | solution.py:125
  106.0 1.9 fusion.53
  109.3 21.2 %all-gather.9.cloned.1.call-done = bf16[64,12,1024]{2,1,0:T(8,128)(2,1)} async-done(((bf16[1,12,1024]{2,1,0:T(8,128)(2,1)}), bf16[64,12,1024]{2,1,0:T(8,128)(2,1)}) %all-gather.9.cloned.1.call-update) | async-done | bytes 1572880 | tf_op jit(solution)/shard_map/all_gather | solution.py:153
  130.5 2.5 reshape.232
  133.1 86.5 %all-gather.5.cloned.1.call-done = bf16[1024,1536]{1,0:T(8,128)(2,1)} async-done(((bf16[16,1536]{1,0:T(8,128)(2,1)}), bf16[1024,1536]{1,0:T(8,128)(2,1)}) %all-gather.5.cloned.1.call-update) | async-done | bytes 3145744 | tf_op jit(solution)/shard_map/all_gather | solution.py:127
  219.6 2.5 convolution_convert_fusion
  226.0 76.6 %all-gather.7.cloned.1.call-done = bf16[512,1024]{1,0:T(8,128)(2,1)} async-done(((bf16[8,1024]{1,0:T(8,128)(2,1)}), bf16[512,1024]{1,0:T(8,128)(2,1)}) %all-gather.7.cloned.1.call-update) | async-done | bytes 1048592 | tf_op jit(solution)/shard_map/all_gather | solution.py:128
  304.7 138.3 %psum.7 = f32[64]{0:T(128)S(1)} all-reduce(f32[64]{0:T(128)S(1)} %multiply_reduce_fusion.3), channel_id=1, replica_groups=mesh['grp'=8,'tile'=64] {'tile'}, use_global_device_ids=true, to_apply=%region_7.0 | all-reduce | flops 64 | bytes 512 | tf_op jit(solution)/shard_map/psum | solution.py:144
  448.4 2.7 fusion.13
  451.1 2.6 fusion.14
  456.6 1.8 dot_general.54
  458.4 3.2 fusion.50
  463.1 23.5 %all_to_all.36 = bf16[64,2,768]{2,1,0:T(2,128)(2,1)S(1)} all-to-all(bf16[64,2,768]{2,1,0:T(2,128)(2,1)S(1)} %reshape.225), channel_id=1, replica_groups=mesh['grp'=8,'tile'=64] {'tile'}, dimensions={0} | all-to-all | bytes 393216 | tf_op jit(solution)/shard_map/all_to_all | solution.py:169
  488.2 1.8 reshape.237
  490.0 19.2 %all_to_all.37 = bf16[1,128,3,256]{3,2,0,1:T(4,128)(2,1)S(1)} all-to-all(bf16[1,128,3,256]{3,2,0,1:T(4,128)(2,1)S(1)} %reshape.237), channel_id=1, replica_groups=mesh['grp'=8,'tile'=64] {'tile'}, dimensions={1} | all-to-all | bytes 393216 | tf_op jit(solution)/shard_map/all_to_all | solution.py:171
  509.7 3.3 collective-permute-start
  512.9 2.1 collective-permute-start.1
  515.7 8.7 %collective-permute-done.1 = bf16[64,1,3,256]{3,1,0,2:T(2,128)(2,1)S(1)} collective-permute-done((bf16[64,1,3,256]{3,1,0,2:T(2,128)(2,1)S(1)}, bf16[64,1,3,256]{3,1,0,2:T(2,128)(2,1)S(1)}, u32[]{:S(2)}, u32[]{:S(2)}) %collective-permute-start.1) | collective-permute-done | bytes 98336 | tf_op jit(solution)/shard_map/ppermute | solution.py:23
  524.4 1.8 select_maximum_fusion
  529.3 3.1 convert_bitcast_fusion
  (95 shorter events, 30.2 us)
Async XLA Ops:
  7.2 123.4 %all-gather.9.cloned.1.call-start = ((), (), s32[]{:S(2)}) async-start(), calls=%async_computation.6 | async-start | bytes 2129920 | tf_op jit(solution)/shard_map/all_gather | solution.py:153
  7.9 211.7 %all-gather.5.cloned.1.call-start = ((), (), s32[]{:S(2)}) async-start(), calls=%async_computation.4 | async-start | bytes 3194880 | tf_op jit(solution)/shard_map/all_gather | solution.py:127
  11.2 35.6 %copy-start.5 = (bf16[12,1024]{1,0:T(8,128)(2,1)S(1)}, bf16[12,1024]{1,0:T(8,128)(2,1)}, u32[]{:S(2)}) copy-start(bf16[12,1024]{1,0:T(8,128)(2,1)} %param.7) | copy-start | bytes 73732
  48.3 56.3 %all-to-all-start.1 = ((bf16[64,12,1024]{2,1,0:T(8,128)(2,1)}), bf16[64,12,1024]{2,1,0:T(8,128)(2,1)S(1)}, u32[]{:S(2)}, u32[]{:S(2)}) async-start(bf16[64,12,1024]{2,1,0:T(8,128)(2,1)} %stack.30), calls=%async_computation.1 | async-start | bytes 4194304 | tf_op jit(solution)/shard_map/all_to_all | solution.py:125
  52.8 249.8 %all-gather.7.cloned.1.call-start = ((), (), s32[]{:S(2)}) async-start(), calls=%async_computation.5 | async-start | bytes 1064960 | tf_op jit(solution)/shard_map/all_gather | solution.py:128
  225.2 0.6 copy-start.11
  225.2 77.4 %copy-start.10 = (f32[2,8,64,64]{2,3,1,0:T(8,128)}, f32[2,8,64,64]{2,3,1,0:T(8,128)S(1)}, u32[]{:S(2)}) copy-start(f32[2,8,64,64]{2,3,1,0:T(8,128)S(1)} %get-tuple-element.16) | copy-start | bytes 786436
  226.0 78.5 %copy-start.6 = (f32[1024]{0:T(1024)S(1)}, f32[1024]{0:T(1024)}, u32[]{:S(2)}) copy-start(f32[1024]{0:T(1024)} %param.10) | copy-start | bytes 12292
  443.8 0.7 copy-start
  447.4 3.7 copy-start.2
  447.4 3.7 copy-start.12
  453.7 1.4 copy-start.3
  453.7 1.4 copy-start.4
  455.1 3.2 copy-start.8
  458.4 3.2 copy-start.1
  488.2 26.9 %copy-start.7 = (bf16[3,3,48,3]{2,3,1,0:T(4,128)(2,1)S(1)}, bf16[3,3,48,3]{2,3,1,0:T(4,128)(2,1)}, u32[]{:S(2)}) copy-start(bf16[3,3,48,3]{2,3,1,0:T(4,128)(2,1)} %param.11) | copy-start | bytes 7780
  488.2 26.9 %copy-start.9 = (f32[64]{0:T(128)S(1)}, f32[64]{0:T(128)}, u32[]{:S(2)}) copy-start(f32[64]{0:T(128)} %get-tuple-element.12) | copy-start | bytes 772
  509.7 6.1 %collective-permute-start = (bf16[64,1,3,256]{3,1,0,2:T(2,128)(2,1)S(1)}, bf16[64,1,3,256]{3,1,0,2:T(2,128)(2,1)S(1)}, u32[]{:S(2)}, u32[]{:S(2)}) collective-permute-start(bf16[64,1,3,256]{3,1,0,2:T(2,128)(2,1)S(1)} %get-tuple-element.7), channel_id=1, source_target_pairs={{0,1},{1,2},{2,3},{3,4},{4,5},{5,6},{6,7},{7,8},{8,9},{9,10},{10,1... | collective-permute-start | bytes 294920 | tf_op jit(solution)/shard_map/ppermute | solution.py:22
  512.9 11.5 %collective-permute-start.1 = (bf16[64,1,3,256]{3,1,0,2:T(2,128)(2,1)S(1)}, bf16[64,1,3,256]{3,1,0,2:T(2,128)(2,1)S(1)}, u32[]{:S(2)}, u32[]{:S(2)}) collective-permute-start(bf16[64,1,3,256]{3,1,0,2:T(2,128)(2,1)S(1)} %get-tuple-element.8), channel_id=1, source_target_pairs={{1,0},{2,1},{3,2},{4,3},{5,4},{6,5},{7,6},{8,7},{9,8},{10,9},{11,1... | collective-permute-start | bytes 294920 | tf_op jit(solution)/shard_map/ppermute | solution.py:23
Sparse Core Ops, SparseCore 0:
  11.3 119.2 all-gather.8
  133.9 85.6 all-gather.4
  222.9 79.6 all-gather.6
